TPU v7x, 512 devices: a whole 4x8x8 slice. The times are simulated.
512 devices in a mesh: bulk: 64 (over x, z, core), span: 8 (over y).
Axes of the slice: x: 4, y: 8, z: 8, core: 2. Of those that a mesh axis runs over, the one named last changes fastest.
Arguments:
- snapshots: float32 [1048576, 128], P(('span', 'bulk'))
- jac_blocks: bfloat16 [8192, 4, 128, 128], P(('span', 'bulk'))
- jac_cols: int32 [8192, 4], P(('span', 'bulk')), may hold values from 0 to 8191, as said below
Outputs:
- modes: float32 [1048576, 128], P(('span', 'bulk'))
- factor: float32 [128, 128], replicated
- jac_modes: bfloat16 [1048576, 128], P(('span', 'bulk'))
- reduced: float32 [128, 128], replicated
Inputs may be any that keep to these rules, and one draw needn't show every extreme that they name: jac_cols[r, 0] = r. Every column block lies in the die region of r (aligned runs of 1024 block rows) and within 16 block rows of the shard of 16 block rows that holds r.
All inputs are finite; a program needn't handle non-finite values.
Results may differ from a plain program's by a relative error of at most 0.0029.
The roundings to bfloat16 on the way count: a program that leaves them out, or rounds other values in their place, can miss the bound.
Values may be sent and summed in bfloat16 or wider, within the bound.
A program may use at most 64 MiB of HBM per device.

v0:
```python
import jax
import jax.numpy as jnp
from jax import lax
from jax.sharding import PartitionSpec as P


def with_halo(array, sides, width):
    for axis, dim in sides:
        size, length = (lax.axis_size(axis), array.shape[dim])
        up = [(i, (i + 1) % size) for i in range(size - 1)]
        down = [(j, i) for i, j in up]
        last = lax.slice_in_dim(array, length - width, length, axis=dim)
        initial = lax.slice_in_dim(array, 0, width, axis=dim)
        before = lax.ppermute(last, axis, up)
        after = lax.ppermute(initial, axis, down)
        array = jnp.concatenate([before, array, after], axis=dim)
    return array


def total_gram(partial_value):
    return lax.psum(partial_value, ("bulk", "span"))


def cholesky_step(data, row_count):
    high = lax.Precision.HIGHEST
    width = data.shape[1]
    partial_value = lax.dot_general(
        data, data, (((0,), (0,)), ((), ())), precision=high, preferred_element_type=jnp.float32
    )
    gram = total_gram(partial_value) / row_count
    lower = jnp.linalg.cholesky(gram)
    inverse = lax.linalg.triangular_solve(
        lower, jnp.eye(width, dtype=jnp.float32), left_side=True, lower=True
    )
    result = jnp.dot(data, inverse.T, precision=high, preferred_element_type=jnp.float32)
    return (result, lower)


def shards(snapshots, jac_blocks, jac_cols):
    high = lax.Precision.HIGHEST
    local_rows, width = snapshots.shape
    block_rows = jac_cols.shape[0]
    blk = jac_blocks.shape[2]
    row_count = local_rows * lax.axis_size(("bulk", "span"))
    first, lower1 = cholesky_step(snapshots, row_count)
    modes, lower2 = cholesky_step(first, row_count)
    factor = jnp.dot(lower2.T, lower1.T, precision=high, preferred_element_type=jnp.float32)
    modes_b = modes.astype(jnp.bfloat16)
    shard_start = (
        lax.axis_index("span") * lax.axis_size("bulk") + lax.axis_index("bulk")
    ) * block_rows
    relative = jac_cols - shard_start
    extended = with_halo(modes_b, (("bulk", 0),), local_rows)
    ext_blocks = extended.reshape(3 * block_rows, blk, width)
    picked = jnp.take(ext_blocks, relative + block_rows, axis=0)
    product = jnp.einsum("rnij,rnjk->rik", jac_blocks, picked, preferred_element_type=jnp.float32)
    jac_modes = product.astype(jnp.bfloat16).reshape(local_rows, width)
    partial_value = lax.dot_general(
        modes,
        jac_modes.astype(jnp.float32),
        (((0,), (0,)), ((), ())),
        precision=high,
        preferred_element_type=jnp.float32,
    )
    reduced = lax.psum(partial_value, ("bulk", "span")) / row_count
    return (modes, factor, jac_modes, reduced)


def solution(mesh):
    return jax.shard_map(
        shards,
        mesh=mesh,
        in_specs=(
            P(("span", "bulk"), None),
            P(("span", "bulk"), None, None, None),
            P(("span", "bulk"), None),
        ),
        out_specs=(P(("span", "bulk"), None), P(), P(("span", "bulk"), None), P()),
        check_vma=False,
    )
```

profile of v0, /device:TPU:1, one launch (start us, length us, event | category | flops | bytes accessed | tf_op | source)
XLA Modules:
  0.0 870.4 jit_solution(4245679873390945482)
XLA Ops:
  7.2 0.0 copy-start
  7.2 0.0 all-reduce.4.cloned.1.call-start
  7.2 4.1 fusion.29
  11.4 0.0 all-reduce.4.cloned.1.call-update
  11.4 0.0 all-reduce.6.cloned.1.call-start
  11.4 266.6 %all-reduce.4.cloned.1.call-done = f32[128,128]{0,1:T(8,128)} async-done(((f32[128,128]{0,1:T(8,128)}), f32[128,128]{0,1:T(8,128)}) %all-reduce.4.cloned.1.call-update) | async-done | bytes 65552 | tf_op jit(solution)/shard_map/psum | solution.py:21
  278.0 0.8 broadcast_multiply_fusion.2
  278.9 0.1 copy.16
  279.0 0.9 fusion.17
  279.8 11.7 %cholesky.44 = f32[128,128]{1,0:T(8,128)S(1)} custom-call(f32[128,128]{1,0:T(8,128)S(1)} %fusion.17), custom_call_target="Cholesky" | custom-call | tf_op jit(solution)/shard_map/jit(cholesky)/cholesky | solution.py:31
  291.6 0.6 compare_reduce_fusion.1
  292.2 0.6 select_bitcast_fusion.1
  292.8 9.8 %custom-call.6 = f32[1,128,128]{1,2,0:T(8,128)S(1)} custom-call(f32[1,128,128]{2,1,0:T(8,128)S(1)} %select_bitcast_fusion.1), custom_call_target="InvertDiagBlocksLowerTriangular" | custom-call | tf_op jit(solution)/shard_map/triangular_solve/custom-call.0 | solution.py:32
  302.6 0.3 fusion.12
  302.9 2.2 fusion.30
  305.1 1.6 fusion.31
  306.8 0.0 all-reduce.6.cloned.1.call-update
  306.8 0.2 all-reduce.8.cloned.1.call-start
  307.0 250.7 %all-reduce.6.cloned.1.call-done = f32[128,128]{0,1:T(8,128)} async-done(((f32[128,128]{0,1:T(8,128)}), f32[128,128]{0,1:T(8,128)}) %all-reduce.6.cloned.1.call-update) | async-done | bytes 65552 | tf_op jit(solution)/shard_map/psum | solution.py:21
  557.7 0.8 broadcast_multiply_fusion.1
  558.5 0.1 copy.18
  558.6 0.9 fusion.15
  559.5 11.7 %cholesky.55 = f32[128,128]{1,0:T(8,128)S(1)} custom-call(f32[128,128]{1,0:T(8,128)S(1)} %fusion.15), custom_call_target="Cholesky" | custom-call | tf_op jit(solution)/shard_map/jit(cholesky)/cholesky | solution.py:31
  571.2 0.7 compare_reduce_fusion
  572.0 0.7 select_bitcast_fusion
  572.7 9.8 %custom-call.7 = f32[1,128,128]{1,2,0:T(8,128)S(1)} custom-call(f32[1,128,128]{2,1,0:T(8,128)S(1)} %select_bitcast_fusion), custom_call_target="InvertDiagBlocksLowerTriangular" | custom-call | tf_op jit(solution)/shard_map/triangular_solve/custom-call.0 | solution.py:32
  582.5 0.3 fusion.10
  582.8 2.9 fusion.28
  585.7 1.9 collective-permute-start.1
  587.6 3.6 collective-permute-start
  591.3 0.0 copy-done.3
  591.3 0.1 copy.20
  591.4 0.1 reshape.36
  591.5 0.1 copy.19
  591.6 4.8 collective-permute-done.1
  596.4 1.3 collective-permute-done
  597.7 2.3 pad_maximum_fusion
  600.0 3.6 gather_fusion
  603.6 0.0 copy-done
  603.6 2.5 fusion.6
  606.0 0.0 copy-start.2
  606.0 0.0 copy-done.1
  606.1 1.4 fusion.32
  607.4 0.0 all-reduce.8.cloned.1.call-update
  607.5 2.2 fusion.19
  609.6 252.7 %all-reduce.8.cloned.1.call-done = f32[128,128]{0,1:T(8,128)} async-done(((f32[128,128]{0,1:T(8,128)}), f32[128,128]{0,1:T(8,128)}) %all-reduce.8.cloned.1.call-update) | async-done | bytes 65552 | tf_op jit(solution)/shard_map/psum | solution.py:65
  862.3 0.8 broadcast_multiply_fusion
  863.2 0.7 copy.22
  (7 shorter events, 0.1 us)
Async XLA Ops:
  7.2 596.4 %copy-start = (bf16[16,4,128,128]{3,2,1,0:T(8,128)(2,1)S(1)}, bf16[16,4,128,128]{3,2,1,0:T(8,128)(2,1)}, u32[]{:S(2)}) copy-start(bf16[16,4,128,128]{3,2,1,0:T(8,128)(2,1)} %param.7) | copy-start | bytes 6291460
  7.2 270.8 %all-reduce.4.cloned.1.call-start = ((), (), s32[]{:S(2)}) async-start(), calls=%async_computation | async-start | bytes 131072 | tf_op jit(solution)/shard_map/psum | solution.py:21
  11.4 546.3 %all-reduce.6.cloned.1.call-start = ((), (), s32[]{:S(2)}) async-start(), calls=%async_computation.1 | async-start | bytes 131072 | tf_op jit(solution)/shard_map/psum | solution.py:21
  306.8 284.5 %copy-start.3 = (s32[16,4]{0,1:T(4,128)S(1)}, s32[16,4]{0,1:T(4,128)}, u32[]{:S(2)}) copy-start(s32[16,4]{0,1:T(4,128)} %param.8) | copy-start | bytes 772
  306.8 555.5 %all-reduce.8.cloned.1.call-start = ((), (), s32[]{:S(2)}) async-start(), calls=%async_computation.2 | async-start | bytes 131072 | tf_op jit(solution)/shard_map/psum | solution.py:65
  585.7 10.7 %collective-permute-start.1 = (bf16[2048,128]{1,0:T(8,128)(2,1)}, bf16[2048,128]{1,0:T(8,128)(2,1)S(1)}, u32[]{:S(2)}, u32[]{:S(2)}) collective-permute-start(bf16[2048,128]{1,0:T(8,128)(2,1)} %get-tuple-element.16), channel_id=1, source_target_pairs={{8,0},{16,8},{24,16},{32,24},{40,32},{48,40},{56,48},{64,56},{72,6... | collective-permute-start | bytes 1572872 | tf_op jit(solution)/shard_map/ppermute | solution.py:15
  587.6 10.1 %collective-permute-start = (bf16[2048,128]{1,0:T(8,128)(2,1)}, bf16[2048,128]{1,0:T(8,128)(2,1)S(1)}, u32[]{:S(2)}, u32[]{:S(2)}) collective-permute-start(bf16[2048,128]{1,0:T(8,128)(2,1)} %get-tuple-element.16), channel_id=1, source_target_pairs={{0,8},{8,16},{16,24},{24,32},{32,40},{40,48},{48,56},{56,64},{64,7... | collective-permute-start | bytes 1572872 | tf_op jit(solution)/shard_map/ppermute | solution.py:14
  603.6 2.5 copy-start.1
  606.0 257.9 %copy-start.2 = (bf16[16,128,128]{1,2,0:T(8,128)(2,1)}, bf16[16,128,128]{1,2,0:T(8,128)(2,1)S(1)}, u32[]{:S(2)}) copy-start(bf16[16,128,128]{1,2,0:T(8,128)(2,1)S(1)} %fusion.6) | copy-start | bytes 1572868
Sparse Core Ops, SparseCore 0:
  13.6 264.4 all-reduce.3
  306.9 250.7 all-reduce.5
  607.6 254.6 all-reduce.7
where the time goes:
time: 871 us; the launch traced here: 870 us
  waiting for transfers between devices  776 us (89%)
  other arithmetic  52.3 us (6%)
  matrix products  17.5 us (2%)
  between operations  13.9 us (2%)
    psum x2, waiting for transfers between devices, total_gram(): return lax.psum(partial_value, ('bulk', 'span'))  517 us
    psum x1, waiting for transfers between devices, shards(): reduced = lax.psum(partial_value, ('bulk', 'span')) / row_count  253 us
    another operation x6, other arithmetic, cholesky_step(): lower = jnp.linalg.cholesky(gram)  24.9 us
    another operation x4, other arithmetic, cholesky_step(): lax.linalg.triangular_solve(lower, jnp.eye(width, dtype=jnp.float32), lef...  20.9 us
  transfers between devices with their start and end apart: 5, of which 5 were waited for; matrix products, arithmetic and copies ran while one was open for 0% of the time, Pallas kernels for 0%

commit v1 on v0

--- a/solution.py
+++ b/solution.py
@@ -62,7 +62,7 @@
         precision=high,
         preferred_element_type=jnp.float32,
     )
-    reduced = lax.psum(partial_value, ("bulk", "span")) / row_count
+    reduced = jnp.sum(lax.all_gather(partial_value, ("bulk", "span")), axis=0) / row_count
     return (modes, factor, jac_modes, reduced)
 
 

time: 871 us -> 786 us (0.902)
  waiting for transfers between devices: 776 us -> 678 us
  other arithmetic: 52.3 us -> 64.6 us
    psum x1 -> x0, waiting for transfers between devices: 253 us -> none  [shards(): reduced = lax.psum(partial_value, ('bulk', 'span')) / row_count]
    all_gather x0 -> x1, waiting for transfers between devices: none -> 155 us  [shards(): lax.all_gather(partial_value, ('bulk', 'span'))]
    reduce_sum x0 -> x1, other arithmetic: none -> 13.1 us  [shards(): jnp.sum(lax.all_gather(partial_value, ('bulk', 'span')), axis=0) / row_count]
where the time goes in v1:
time: 786 us; the launch traced here: 785 us
  waiting for transfers between devices  678 us (86%)
  other arithmetic  64.6 us (8%)
  matrix products  17.8 us (2%)
  between operations  13.9 us (2%)
    psum x2, waiting for transfers between devices, total_gram(): return lax.psum(partial_value, ('bulk', 'span'))  517 us
    all_gather x1, waiting for transfers between devices, shards(): lax.all_gather(partial_value, ('bulk', 'span'))  155 us
    another operation x6, other arithmetic, cholesky_step(): lower = jnp.linalg.cholesky(gram)  24.9 us
    another operation x4, other arithmetic, cholesky_step(): lax.linalg.triangular_solve(lower, jnp.eye(width, dtype=jnp.float32), lef...  20.9 us
  transfers between devices with their start and end apart: 5, of which 5 were waited for; matrix products, arithmetic and copies ran while one was open for 0% of the time, Pallas kernels for 0%

profile of v1, /device:TPU:1, one launch (start us, length us, event | category | flops | bytes accessed | tf_op | source)
XLA Modules:
  0.0 785.4 jit_solution(4662453676478478288)
XLA Ops:
  7.2 0.0 copy-start
  7.2 0.0 all-reduce.3.cloned.1.call-start
  7.2 4.1 fusion.29
  11.4 0.0 all-reduce.3.cloned.1.call-update
  11.4 0.0 all-reduce.5.cloned.1.call-start
  11.4 266.6 %all-reduce.3.cloned.1.call-done = f32[128,128]{0,1:T(8,128)} async-done(((f32[128,128]{0,1:T(8,128)}), f32[128,128]{0,1:T(8,128)}) %all-reduce.3.cloned.1.call-update) | async-done | bytes 65552 | tf_op jit(solution)/shard_map/psum | solution.py:21
  278.0 0.8 broadcast_multiply_fusion.2
  278.9 0.1 copy.22
  279.0 0.9 fusion.17
  279.8 11.7 %cholesky.44 = f32[128,128]{1,0:T(8,128)S(1)} custom-call(f32[128,128]{1,0:T(8,128)S(1)} %fusion.17), custom_call_target="Cholesky" | custom-call | tf_op jit(solution)/shard_map/jit(cholesky)/cholesky | solution.py:31
  291.6 0.7 compare_reduce_fusion.1
  292.3 0.7 select_bitcast_fusion.1
  293.0 9.8 %custom-call.6 = f32[1,128,128]{1,2,0:T(8,128)S(1)} custom-call(f32[1,128,128]{2,1,0:T(8,128)S(1)} %select_bitcast_fusion.1), custom_call_target="InvertDiagBlocksLowerTriangular" | custom-call | tf_op jit(solution)/shard_map/triangular_solve/custom-call.0 | solution.py:32
  302.8 0.3 fusion.12
  303.1 2.2 fusion.30
  305.3 1.6 fusion.31
  306.9 0.0 all-reduce.5.cloned.1.call-update
  307.0 0.2 all-gather.3.cloned.1.call-start
  307.2 250.7 %all-reduce.5.cloned.1.call-done = f32[128,128]{0,1:T(8,128)} async-done(((f32[128,128]{0,1:T(8,128)}), f32[128,128]{0,1:T(8,128)}) %all-reduce.5.cloned.1.call-update) | async-done | bytes 65552 | tf_op jit(solution)/shard_map/psum | solution.py:21
  557.9 0.8 broadcast_multiply_fusion.1
  558.8 0.1 copy.24
  558.9 0.9 fusion.15
  559.7 11.7 %cholesky.55 = f32[128,128]{1,0:T(8,128)S(1)} custom-call(f32[128,128]{1,0:T(8,128)S(1)} %fusion.15), custom_call_target="Cholesky" | custom-call | tf_op jit(solution)/shard_map/jit(cholesky)/cholesky | solution.py:31
  571.5 0.7 compare_reduce_fusion
  572.1 0.6 select_bitcast_fusion
  572.8 9.8 %custom-call.7 = f32[1,128,128]{1,2,0:T(8,128)S(1)} custom-call(f32[1,128,128]{2,1,0:T(8,128)S(1)} %select_bitcast_fusion), custom_call_target="InvertDiagBlocksLowerTriangular" | custom-call | tf_op jit(solution)/shard_map/triangular_solve/custom-call.0 | solution.py:32
  582.6 0.3 fusion.10
  582.9 2.9 fusion.28
  585.8 1.9 collective-permute-start.1
  587.7 3.6 collective-permute-start
  591.4 0.0 copy-done.3
  591.4 0.1 copy.25
  591.5 0.1 copy.26
  591.6 0.1 reshape.36
  591.7 4.8 collective-permute-done.1
  596.5 1.3 collective-permute-done
  597.8 2.3 pad_maximum_fusion
  600.1 3.6 gather_fusion
  603.7 0.0 copy-done
  603.7 2.5 fusion.6
  606.2 0.0 copy-start.2
  606.2 1.7 fusion.32
  607.9 0.0 all-gather.3.cloned.1.call-update
  607.9 2.2 fusion.19
  610.1 154.9 %all-gather.3.cloned.1.call-done = f32[65536,128]{1,0:T(8,128)} async-done(((f32[128,128]{1,0:T(8,128)}), f32[65536,128]{1,0:T(8,128)}) %all-gather.3.cloned.1.call-update) | async-done | bytes 33554448 | tf_op jit(solution)/shard_map/all_gather | solution.py:65
  764.9 13.1 %reduce_sum.9 = f32[128,128]{1,0:T(8,128)S(1)} reduce(f32[512,128,128]{2,1,0:T(8,128)} %bitcast.40, f32[]{:T(128)} %constant.65.clone.1), dimensions={0}, to_apply=%region_4.7 | reduce | flops 8372224 | bytes 33619972 | tf_op jit(solution)/shard_map/reduce_sum | solution.py:65
  778.0 0.1 copy.27
  778.1 0.7 copy.28
  (9 shorter events, 0.1 us)
Async XLA Ops:
  7.2 596.5 %copy-start = (bf16[16,4,128,128]{3,2,1,0:T(8,128)(2,1)S(1)}, bf16[16,4,128,128]{3,2,1,0:T(8,128)(2,1)}, u32[]{:S(2)}) copy-start(bf16[16,4,128,128]{3,2,1,0:T(8,128)(2,1)} %param.7) | copy-start | bytes 6291460
  7.2 270.8 %all-reduce.3.cloned.1.call-start = ((), (), s32[]{:S(2)}) async-start(), calls=%async_computation | async-start | bytes 131072 | tf_op jit(solution)/shard_map/psum | solution.py:21
  11.4 546.5 %all-reduce.5.cloned.1.call-start = ((), (), s32[]{:S(2)}) async-start(), calls=%async_computation.1 | async-start | bytes 131072 | tf_op jit(solution)/shard_map/psum | solution.py:21
  306.9 284.5 %copy-start.3 = (s32[16,4]{0,1:T(4,128)S(1)}, s32[16,4]{0,1:T(4,128)}, u32[]{:S(2)}) copy-start(s32[16,4]{0,1:T(4,128)} %param.8) | copy-start | bytes 772
  307.0 458.0 %all-gather.3.cloned.1.call-start = ((), (), s32[]{:S(2)}) async-start(), calls=%async_computation.2 | async-start | bytes 33619968 | tf_op jit(solution)/shard_map/all_gather | solution.py:65
  585.8 10.7 %collective-permute-start.1 = (bf16[2048,128]{1,0:T(8,128)(2,1)}, bf16[2048,128]{1,0:T(8,128)(2,1)S(1)}, u32[]{:S(2)}, u32[]{:S(2)}) collective-permute-start(bf16[2048,128]{1,0:T(8,128)(2,1)} %get-tuple-element.20), channel_id=1, source_target_pairs={{8,0},{16,8},{24,16},{32,24},{40,32},{48,40},{56,48},{64,56},{72,6... | collective-permute-start | bytes 1572872 | tf_op jit(solution)/shard_map/ppermute | solution.py:15
  587.7 10.1 %collective-permute-start = (bf16[2048,128]{1,0:T(8,128)(2,1)}, bf16[2048,128]{1,0:T(8,128)(2,1)S(1)}, u32[]{:S(2)}, u32[]{:S(2)}) collective-permute-start(bf16[2048,128]{1,0:T(8,128)(2,1)} %get-tuple-element.20), channel_id=1, source_target_pairs={{0,8},{8,16},{16,24},{24,32},{32,40},{40,48},{48,56},{56,64},{64,7... | collective-permute-start | bytes 1572872 | tf_op jit(solution)/shard_map/ppermute | solution.py:14
  603.7 2.5 copy-start.1
  606.2 171.9 %copy-start.2 = (bf16[16,128,128]{1,2,0:T(8,128)(2,1)}, bf16[16,128,128]{1,2,0:T(8,128)(2,1)S(1)}, u32[]{:S(2)}) copy-start(bf16[16,128,128]{1,2,0:T(8,128)(2,1)S(1)} %fusion.6) | copy-start | bytes 1572868
Sparse Core Ops, SparseCore 0:
  13.6 264.4 all-reduce.2
  307.1 250.7 all-reduce.4
  608.0 156.8 all-gather.2

commit v2 on v0

--- a/solution.py
+++ b/solution.py
@@ -62,7 +62,7 @@
         precision=high,
         preferred_element_type=jnp.float32,
     )
-    reduced = lax.psum(partial_value, ("bulk", "span")) / row_count
+    reduced = lax.psum(lax.psum(partial_value, "bulk"), "span") / row_count
     return (modes, factor, jac_modes, reduced)
 
 

time: 871 us -> 865 us (level)
  waiting for transfers between devices: 776 us -> 767 us
    psum x1 -> x2, waiting for transfers between devices: 253 us -> 243 us  [shards(): reduced = lax.psum(lax.psum(partial_value, 'bulk'), 'span') / row_count]
  transfers between devices with their start and end apart: 5 -> 6, of which waited for: 5 -> 6; matrix products, arithmetic and copies ran while one was open for 0% -> 0% of each run, Pallas kernels for 0% -> 0%
where the time goes in v2:
time: 865 us; the launch traced here: 861 us
  waiting for transfers between devices  767 us (89%)
  other arithmetic  52.3 us (6%)
  matrix products  17.5 us (2%)
  between operations  13.9 us (2%)
    psum x2, waiting for transfers between devices, total_gram(): return lax.psum(partial_value, ('bulk', 'span'))  517 us
    psum x2, waiting for transfers between devices, shards(): reduced = lax.psum(lax.psum(partial_value, 'bulk'), 'span') / row_count  243 us
    another operation x6, other arithmetic, cholesky_step(): lower = jnp.linalg.cholesky(gram)  24.9 us
    another operation x4, other arithmetic, cholesky_step(): lax.linalg.triangular_solve(lower, jnp.eye(width, dtype=jnp.float32), lef...  20.9 us
  transfers between devices with their start and end apart: 6, of which 6 were waited for; matrix products, arithmetic and copies ran while one was open for 0% of the time, Pallas kernels for 0%

profile of v2, /device:TPU:1, one launch (start us, length us, event | category | flops | bytes accessed | tf_op | source)
XLA Modules:
  0.0 861.0 jit_solution(17949244246582807750)
XLA Ops:
  7.2 0.0 copy-start
  7.2 0.0 all-reduce.5.cloned.1.call-start
  7.2 4.1 fusion.29
  11.4 0.0 all-reduce.5.cloned.1.call-update
  11.4 0.0 all-reduce.7.cloned.1.call-start
  11.4 266.6 %all-reduce.5.cloned.1.call-done = f32[128,128]{0,1:T(8,128)} async-done(((f32[128,128]{0,1:T(8,128)}), f32[128,128]{0,1:T(8,128)}) %all-reduce.5.cloned.1.call-update) | async-done | bytes 65552 | tf_op jit(solution)/shard_map/psum | solution.py:21
  278.0 0.8 broadcast_multiply_fusion.2
  278.9 0.1 copy.16
  279.0 0.9 fusion.17
  279.8 11.7 %cholesky.44 = f32[128,128]{1,0:T(8,128)S(1)} custom-call(f32[128,128]{1,0:T(8,128)S(1)} %fusion.17), custom_call_target="Cholesky" | custom-call | tf_op jit(solution)/shard_map/jit(cholesky)/cholesky | solution.py:31
  291.6 0.6 compare_reduce_fusion.1
  292.2 0.6 select_bitcast_fusion.1
  292.8 9.8 %custom-call.6 = f32[1,128,128]{1,2,0:T(8,128)S(1)} custom-call(f32[1,128,128]{2,1,0:T(8,128)S(1)} %select_bitcast_fusion.1), custom_call_target="InvertDiagBlocksLowerTriangular" | custom-call | tf_op jit(solution)/shard_map/triangular_solve/custom-call.0 | solution.py:32
  302.6 0.3 fusion.12
  302.9 2.2 fusion.30
  305.1 1.6 fusion.31
  306.8 0.0 all-reduce.7.cloned.1.call-update
  306.8 0.2 all-reduce.9.cloned.1.call-start
  307.0 250.7 %all-reduce.7.cloned.1.call-done = f32[128,128]{0,1:T(8,128)} async-done(((f32[128,128]{0,1:T(8,128)}), f32[128,128]{0,1:T(8,128)}) %all-reduce.7.cloned.1.call-update) | async-done | bytes 65552 | tf_op jit(solution)/shard_map/psum | solution.py:21
  557.7 0.8 broadcast_multiply_fusion.1
  558.5 0.1 copy.18
  558.6 0.9 fusion.15
  559.5 11.7 %cholesky.55 = f32[128,128]{1,0:T(8,128)S(1)} custom-call(f32[128,128]{1,0:T(8,128)S(1)} %fusion.15), custom_call_target="Cholesky" | custom-call | tf_op jit(solution)/shard_map/jit(cholesky)/cholesky | solution.py:31
  571.2 0.7 compare_reduce_fusion
  572.0 0.7 select_bitcast_fusion
  572.7 9.8 %custom-call.7 = f32[1,128,128]{1,2,0:T(8,128)S(1)} custom-call(f32[1,128,128]{2,1,0:T(8,128)S(1)} %select_bitcast_fusion), custom_call_target="InvertDiagBlocksLowerTriangular" | custom-call | tf_op jit(solution)/shard_map/triangular_solve/custom-call.0 | solution.py:32
  582.5 0.3 fusion.10
  582.8 2.9 fusion.28
  585.7 1.9 collective-permute-start.1
  587.6 3.6 collective-permute-start
  591.3 0.1 copy.20
  591.4 0.1 reshape.36
  591.5 0.1 copy.19
  591.6 4.8 collective-permute-done.1
  596.4 1.3 collective-permute-done
  597.7 2.3 pad_maximum_fusion
  600.0 3.6 gather_fusion
  603.6 2.5 fusion.6
  606.0 0.0 copy-start.2
  606.1 1.4 fusion.32
  607.4 0.0 all-reduce.9.cloned.1.call-update
  607.5 0.0 all-reduce.11.cloned.1.call-start
  607.5 175.3 %all-reduce.9.cloned.1.call-done = f32[128,128]{0,1:T(8,128)} async-done(((f32[128,128]{0,1:T(8,128)}), f32[128,128]{0,1:T(8,128)}) %all-reduce.9.cloned.1.call-update) | async-done | bytes 65552 | tf_op jit(solution)/shard_map/psum | solution.py:65
  782.8 0.0 all-reduce.11.cloned.1.call-update
  782.8 2.2 fusion.19
  785.0 67.9 %all-reduce.11.cloned.1.call-done = f32[128,128]{0,1:T(8,128)} async-done(((f32[128,128]{0,1:T(8,128)}), f32[128,128]{0,1:T(8,128)}) %all-reduce.11.cloned.1.call-update) | async-done | bytes 65552 | tf_op jit(solution)/shard_map/psum | solution.py:65
  852.9 0.8 broadcast_multiply_fusion
  853.7 0.7 copy.22
  (10 shorter events, 0.1 us)
Async XLA Ops:
  7.2 596.4 %copy-start = (bf16[16,4,128,128]{3,2,1,0:T(8,128)(2,1)S(1)}, bf16[16,4,128,128]{3,2,1,0:T(8,128)(2,1)}, u32[]{:S(2)}) copy-start(bf16[16,4,128,128]{3,2,1,0:T(8,128)(2,1)} %param.7) | copy-start | bytes 6291460
  7.2 270.8 %all-reduce.5.cloned.1.call-start = ((), (), s32[]{:S(2)}) async-start(), calls=%async_computation | async-start | bytes 131072 | tf_op jit(solution)/shard_map/psum | solution.py:21
  11.4 546.3 %all-reduce.7.cloned.1.call-start = ((), (), s32[]{:S(2)}) async-start(), calls=%async_computation.1 | async-start | bytes 131072 | tf_op jit(solution)/shard_map/psum | solution.py:21
  306.8 284.5 %copy-start.3 = (s32[16,4]{0,1:T(4,128)S(1)}, s32[16,4]{0,1:T(4,128)}, u32[]{:S(2)}) copy-start(s32[16,4]{0,1:T(4,128)} %param.8) | copy-start | bytes 772
  306.8 476.0 %all-reduce.9.cloned.1.call-start = ((), (), s32[]{:S(2)}) async-start(), calls=%async_computation.2 | async-start | bytes 131072 | tf_op jit(solution)/shard_map/psum | solution.py:65
  585.7 10.7 %collective-permute-start.1 = (bf16[2048,128]{1,0:T(8,128)(2,1)}, bf16[2048,128]{1,0:T(8,128)(2,1)S(1)}, u32[]{:S(2)}, u32[]{:S(2)}) collective-permute-start(bf16[2048,128]{1,0:T(8,128)(2,1)} %get-tuple-element.16), channel_id=1, source_target_pairs={{8,0},{16,8},{24,16},{32,24},{40,32},{48,40},{56,48},{64,56},{72,6... | collective-permute-start | bytes 1572872 | tf_op jit(solution)/shard_map/ppermute | solution.py:15
  587.6 10.1 %collective-permute-start = (bf16[2048,128]{1,0:T(8,128)(2,1)}, bf16[2048,128]{1,0:T(8,128)(2,1)S(1)}, u32[]{:S(2)}, u32[]{:S(2)}) collective-permute-start(bf16[2048,128]{1,0:T(8,128)(2,1)} %get-tuple-element.16), channel_id=1, source_target_pairs={{0,8},{8,16},{16,24},{24,32},{32,40},{40,48},{48,56},{56,64},{64,7... | collective-permute-start | bytes 1572872 | tf_op jit(solution)/shard_map/ppermute | solution.py:14
  603.6 2.5 copy-start.1
  606.0 248.4 %copy-start.2 = (bf16[16,128,128]{1,2,0:T(8,128)(2,1)}, bf16[16,128,128]{1,2,0:T(8,128)(2,1)S(1)}, u32[]{:S(2)}) copy-start(bf16[16,128,128]{1,2,0:T(8,128)(2,1)S(1)} %fusion.6) | copy-start | bytes 1572868
  607.5 245.4 %all-reduce.11.cloned.1.call-start = ((), (), s32[]{:S(2)}) async-start(), calls=%async_computation.3 | async-start | bytes 131072 | tf_op jit(solution)/shard_map/psum | solution.py:65
Sparse Core Ops, SparseCore 0:
  13.6 264.4 all-reduce.4
  306.9 250.7 all-reduce.6
  607.6 175.1 all-reduce.8
  785.0 67.8 all-reduce.10
